TPU v7x, 32 devices: a whole 2x2x4 slice. The times are simulated.
32 devices in a mesh: grp: 8 (over z, y), blk: 4 (over x, core).
Axes of the slice: x: 2, y: 2, z: 4, core: 2. Of those that a mesh axis runs over, the one named last changes fastest.
Arguments:
- field_phase: float32 [6, 16384], P(None, ('grp', 'blk')), may hold values from -10 to 10
- field_mass: float32 [16384], P(('grp', 'blk')), may hold values from 0.2 to 5
- old_force: float32 [6, 2048], P(None, ('grp', 'blk')), may hold values from -6 to 6
- target_slot: int32 [101, 2048], P(None, ('grp', 'blk')), may hold values from 0 to 12927, as said below
- target_star: int32 [101, 2048], P(None, ('grp', 'blk')), may hold values from 0 to 511
Outputs:
- reg_force: float32 [6, 2048], P(None, ('grp', 'blk'))
- irr_force: float32 [6, 2048], P(None, ('grp', 'blk'))
- new_state: float32 [6, 2048], P(None, ('grp', 'blk'))
Inputs may be any that keep to these rules, and one draw needn't show every extreme that they name: `target_slot`: within the 64 columns of one device all slots differ; slot // 404 is the index, grp-major over grp and blk, of the device that holds the star, so at most 404 entries of one device go to one owner, and some owners receive exactly 404 from every device.
All inputs are finite; a program needn't handle non-finite values.
Results may differ from a plain program's by a relative error of at most 0.0003.
Values sent between devices are 32-bit elements; how exact they have to be, the bound alone decides.
No kernel may reach another device: no remote copies, remote signals or barrier semaphores. Data moves between devices by JAX's collectives and lax.ppermute only.
A program may use at most 128 MiB of HBM per device.

v0:
```python
import math
import jax
import jax.numpy as jnp
from jax import lax
from jax.sharding import PartitionSpec as P

soften_sq = 0.01
step_length = 0.5


def passed_along(x, axis, by):
    count = lax.axis_size(axis)
    return lax.ppermute(x, axis, [(i, (i + by) % count) for i in range(count)])


def pair_block(receivers, emitters):
    separation = emitters[0:3, None, :] - receivers[0:3, :, None]
    rel_velocity = emitters[3:6, None, :] - receivers[3:6, :, None]
    dist_sq = soften_sq + jnp.sum(separation * separation, axis=0)
    inverse = lax.rsqrt(dist_sq)
    weight = emitters[6][None, :] * inverse * inverse * inverse
    radial = 3.0 * jnp.sum(separation * rel_velocity, axis=0) / dist_sq
    pull_sum = jnp.sum(weight[None] * separation, axis=2)
    jerk_sum = jnp.sum(weight[None] * (rel_velocity - radial[None] * separation), axis=2)
    return jnp.concatenate([pull_sum, jerk_sum], axis=0)


def pair_sum(receivers, emitters):
    row_total = receivers.shape[1]
    tile_rows = math.gcd(row_total, 256)
    tiles = receivers.reshape(6, row_total // tile_rows, tile_rows).transpose(1, 0, 2)
    emit_total = emitters.shape[1]
    emit_rows = math.gcd(emit_total, 1024)
    emit_blocks = emitters.reshape(7, emit_total // emit_rows, emit_rows).transpose(1, 0, 2)

    def single_tile(block_rows):

        def add_block(total, emit_piece):
            return (total + pair_block(block_rows, emit_piece), None)

        start = jnp.zeros((6, tile_rows), jnp.float32)
        total, unused = lax.scan(add_block, start, emit_blocks)
        return total

    result = lax.map(single_tile, tiles)
    return result.transpose(1, 0, 2).reshape(6, row_total)


def neighbour_sum(receivers, emitters):
    separation = emitters[0:3] - receivers[0:3, None, :]
    rel_velocity = emitters[3:6] - receivers[3:6, None, :]
    dist_sq = soften_sq + jnp.sum(separation * separation, axis=0)
    inverse = lax.rsqrt(dist_sq)
    weight = emitters[6] * inverse * inverse * inverse
    radial = 3.0 * jnp.sum(separation * rel_velocity, axis=0) / dist_sq
    pull_sum = jnp.sum(weight[None] * separation, axis=1)
    jerk_sum = jnp.sum(weight[None] * (rel_velocity - radial[None] * separation), axis=1)
    return jnp.concatenate([pull_sum, jerk_sum], axis=0)


def corrector(home_state, regular, irregular, old_force):
    accel_new = regular[0:3] + irregular[0:3]
    jerk_new = regular[3:6] + irregular[3:6]
    difference = old_force[0:3] - accel_new
    snap_term = -6.0 * difference - step_length * (4.0 * old_force[3:6] + 2.0 * jerk_new)
    crackle_term = 12.0 * difference + 6.0 * step_length * (old_force[3:6] + jerk_new)
    step_square = step_length * step_length
    position = home_state[0:3] + step_square / 24.0 * snap_term + step_square / 120.0 * crackle_term
    velocity = home_state[3:6] + step_length / 6.0 * snap_term + step_length / 24.0 * crackle_term
    return jnp.concatenate([position, velocity], axis=0)


def per_device(field_phase, field_mass, old_force, target_slot, target_star):
    target_cols = target_slot.shape[0]
    active_rows = target_slot.shape[1]
    group_count = lax.axis_size("grp")
    loop_count = lax.axis_size("blk")
    device_count = group_count * loop_count
    local_stars = field_phase.shape[1]
    star_total = local_stars * device_count
    star_table = jnp.concatenate([field_phase, field_mass[None, :]], axis=0)
    target_count = target_cols * active_rows
    bucket_size = 2 * ((target_count + device_count - 1) // device_count)
    slot_flat = target_slot.reshape(target_count)
    star_flat = target_star.reshape(target_count)
    global_id = slot_flat // bucket_size * local_stars + star_flat
    shard_rows = lax.all_gather(star_table, ("grp", "blk"), axis=1, tiled=True)
    inside = (global_id >= 0) & (global_id < shard_rows.shape[1])
    picked = jnp.take(shard_rows, jnp.clip(global_id, 0, shard_rows.shape[1] - 1), axis=1)
    fetched = jnp.where(inside[None, :], picked, 0.0)
    fetched = fetched.reshape(7, target_cols, active_rows)
    own_state = fetched[0:6, 0, :]
    irregular = neighbour_sum(own_state, fetched[:, 1:, :]) / (target_cols - 1)
    group_block = lax.all_gather(own_state, "grp", axis=1, tiled=True)
    running = jnp.zeros_like(group_block)
    moving = group_block
    for circuit in range(loop_count):
        running = running + pair_sum(moving, star_table)
        parcel = passed_along(jnp.concatenate([moving, running], axis=0), "blk", 1)
        moving = parcel[0:6]
        running = parcel[6:12]
    row_offset = lax.axis_index("grp") * active_rows
    home_state = lax.dynamic_slice_in_dim(moving, row_offset, active_rows, 1)
    summed = lax.psum(running, "grp")
    regular = lax.dynamic_slice_in_dim(summed, row_offset, active_rows, 1)
    regular = regular / star_total
    return (regular, irregular, corrector(home_state, regular, irregular, old_force))


def solution(mesh):
    in_specs = (
        P(None, ("grp", "blk")),
        P(("grp", "blk")),
        P(None, ("grp", "blk")),
        P(None, ("grp", "blk")),
        P(None, ("grp", "blk")),
    )
    out_specs = (P(None, ("grp", "blk")), P(None, ("grp", "blk")), P(None, ("grp", "blk")))
    return jax.shard_map(
        per_device, mesh=mesh, in_specs=in_specs, out_specs=out_specs, check_vma=False
    )
```

profile of v0, /device:TPU:0, one launch (start us, length us, event | category | flops | bytes accessed | tf_op | source)
XLA Modules:
  0.0 220.9 jit_solution(7027107915442283614)
XLA Ops:
  0.6 0.8 broadcast_divide_fusion
  1.4 1.4 compare_and_fusion.1
  2.8 0.9 copy.91
  3.8 1.4 compare_and_fusion
  5.2 0.7 pad_maximum_fusion.4
  6.0 0.7 fusion.33
  7.1 0.1 fusion.28
  7.4 101.1 %all_gather.6 = f32[7,16384]{0,1:T(8,128)} all-gather(f32[7,512]{0,1:T(8,128)S(1)} %copy.88), channel_id=1, replica_groups=mesh['grp'=8,'blk'=4] {'grp','blk'}, dimensions={1}, use_global_device_ids=true | all-gather | bytes 473088 | tf_op jit(solution)/shard_map/all_gather | solution.py:87
  108.5 13.9 %gather_fusion = f32[6464,7]{1,0:T(8,128)S(1)} fusion(f32[7,16384]{0,1:T(8,128)} %all_gather.6, s32[7168]{0:T(1024)S(1)} %pad_clamp_fusion), kind=kCustom, calls=%fused_computation | custom fusion | bytes 387840 | tf_op jit(solution)/shard_map/jit(_take)/gather | solution.py:89
  122.4 2.1 copy.92
  124.5 0.7 select_select_fusion
  125.2 0.5 copy.93
  125.7 33.6 %all-gather = f32[6,1,512]{0,1,2:T(1,128)S(1)} all-gather(f32[6,1,64]{0,1,2:T(1,128)S(1)} %copy.93), channel_id=2, replica_groups=mesh['grp'=8,'blk'=4] {'grp'}, dimensions={2}, use_global_device_ids=true | all-gather | bytes 13824 | tf_op jit(solution)/shard_map/all_gather | solution.py:94
  159.5 2.7 %while.36 = (s32[]{:T(128)}, f32[2,6,256]{2,1,0:T(8,128)S(1)}, f32[1,7,512]{2,1,0:T(8,128)S(1)}, f32[2,6,256]{2,0,1:T(2,128)S(1)}, s32[]{:T(128)}, /*index=5*/s32[]{:T(128)}, s32[]{}) while((s32[]{:T(128)}, f32[2,6,256]{2,1,0:T(8,128)S(1)}, f32[1,7,512]{2,1,0:T(8,128)S(1)}, f32[2,6,256]{2,0,1:T(2,128)S(1)}, s32[]{:T(128)}, ...), condition=%wide.region_5.6_spmd, body=%wide.region_0.5_spmd.sunk | while | flops 6029315 | bytes 4309093 | solution.py:45
  159.6 0.4 fusion.46
  160.1 0.7 fusion.47
  160.9 0.4 fusion.46
  161.3 0.1 multiply_divide_fusion.9
  161.5 0.7 fusion.47
  162.4 0.2 multiply_reduce_fusion.3
  162.6 3.0 %collective-permute-done = f32[12,512]{1,0:T(8,128)S(1)} collective-permute-done((f32[12,512]{1,0:T(8,128)S(1)}, f32[12,512]{1,0:T(8,128)S(1)}, u32[]{:S(2)}, u32[]{:S(2)}) %collective-permute-start) | collective-permute-done | bytes 24608 | tf_op jit(solution)/shard_map/ppermute | solution.py:13
  165.6 2.7 %while.37 = (s32[]{:T(128)}, f32[2,6,256]{2,1,0:T(8,128)S(1)}, f32[1,7,512]{2,1,0:T(8,128)S(1)}, f32[2,6,256]{2,1,0:T(8,128)S(1)}, s32[]{:T(128)}, /*index=5*/s32[]{:T(128)}, s32[]{}) while((s32[]{:T(128)}, f32[2,6,256]{2,1,0:T(8,128)S(1)}, f32[1,7,512]{2,1,0:T(8,128)S(1)}, f32[2,6,256]{2,1,0:T(8,128)S(1)}, s32[]{:T(128)}, ...), condition=%wide.region_11.12_spmd, body=%wide.region_6.11_spmd.sunk | while | flops 6029315 | bytes 4296805 | solution.py:45
  165.7 0.4 fusion.49
  166.1 0.1 multiply_divide_fusion.10
  166.2 0.7 fusion.50
  167.0 0.4 fusion.49
  167.4 0.1 multiply_divide_fusion.10
  167.6 0.7 fusion.50
  168.4 1.5 collective-permute-start.1
  169.9 1.8 collective-permute-done.1
  171.8 2.7 %while.38 = (s32[]{:T(128)}, f32[2,6,256]{2,1,0:T(8,128)S(1)}, f32[1,7,512]{2,1,0:T(8,128)S(1)}, f32[2,6,256]{2,1,0:T(8,128)S(1)}, s32[]{:T(128)}, /*index=5*/s32[]{:T(128)}, s32[]{}) while((s32[]{:T(128)}, f32[2,6,256]{2,1,0:T(8,128)S(1)}, f32[1,7,512]{2,1,0:T(8,128)S(1)}, f32[2,6,256]{2,1,0:T(8,128)S(1)}, s32[]{:T(128)}, ...), condition=%wide.region_17.18_spmd, body=%wide.region_12.17_spmd.sunk | while | flops 6029315 | bytes 4296805 | solution.py:45
  171.8 0.4 fusion.52
  172.2 0.1 multiply_divide_fusion.11
  172.3 0.7 fusion.53
  173.1 0.4 fusion.52
  173.7 0.7 fusion.53
  174.5 1.5 collective-permute-start.2
  176.0 1.9 collective-permute-done.2
  177.9 2.7 %while.39 = (s32[]{:T(128)}, f32[2,6,256]{2,1,0:T(8,128)S(1)}, f32[1,7,512]{2,1,0:T(8,128)S(1)}, f32[2,6,256]{2,1,0:T(8,128)S(1)}, s32[]{:T(128)}, /*index=5*/s32[]{:T(128)}, s32[]{}) while((s32[]{:T(128)}, f32[2,6,256]{2,1,0:T(8,128)S(1)}, f32[1,7,512]{2,1,0:T(8,128)S(1)}, f32[2,6,256]{2,1,0:T(8,128)S(1)}, s32[]{:T(128)}, ...), condition=%wide.region_23.24_spmd, body=%wide.region_18.23_spmd.sunk | while | flops 6029315 | bytes 4296805 | solution.py:45
  177.9 0.4 fusion.55
  178.5 0.7 fusion.56
  179.3 0.4 fusion.55
  179.8 0.7 fusion.56
  180.6 1.5 collective-permute-start.3
  182.1 0.2 multiply_reduce_fusion.2
  182.3 1.7 collective-permute-done.3
  184.0 36.1 %psum.7 = f32[6,512]{1,0:T(8,128)S(1)} all-reduce(f32[6,512]{1,0:T(8,128)S(1)} %get-tuple-element.289), channel_id=1, replica_groups=mesh['grp'=8,'blk'=4] {'grp'}, use_global_device_ids=true, to_apply=%region_24.25 | all-reduce | flops 3072 | bytes 24576 | tf_op jit(solution)/shard_map/psum | solution.py:104
  220.3 0.6 pad_maximum_fusion.5
  (77 shorter events, 2.2 us)
Async XLA Ops:
  162.3 3.4 %collective-permute-start = (f32[12,512]{1,0:T(8,128)S(1)}, f32[12,512]{1,0:T(8,128)S(1)}, u32[]{:S(2)}, u32[]{:S(2)}) collective-permute-start(f32[12,512]{1,0:T(8,128)S(1)} %pad_maximum_fusion), channel_id=1, source_target_pairs={{0,1},{1,2},{2,3},{3,0},{4,5},{5,6},{6,7},{7,4},{8,9},{9,10},{10,1... | collective-permute-start | bytes 73736 | tf_op jit(solution)/shard_map/ppermute | solution.py:13
  168.4 3.4 %collective-permute-start.1 = (f32[12,512]{1,0:T(8,128)S(1)}, f32[12,512]{1,0:T(8,128)S(1)}, u32[]{:S(2)}, u32[]{:S(2)}) collective-permute-start(f32[12,512]{1,0:T(8,128)S(1)} %pad_maximum_fusion.1), channel_id=1, source_target_pairs={{0,1},{1,2},{2,3},{3,0},{4,5},{5,6},{6,7},{7,4},{8,9},{9,10},{10,1... | collective-permute-start | bytes 73736 | tf_op jit(solution)/shard_map/ppermute | solution.py:13
  174.5 3.4 %collective-permute-start.2 = (f32[12,512]{1,0:T(8,128)S(1)}, f32[12,512]{1,0:T(8,128)S(1)}, u32[]{:S(2)}, u32[]{:S(2)}) collective-permute-start(f32[12,512]{1,0:T(8,128)S(1)} %pad_maximum_fusion.2), channel_id=1, source_target_pairs={{0,1},{1,2},{2,3},{3,0},{4,5},{5,6},{6,7},{7,4},{8,9},{9,10},{10,1... | collective-permute-start | bytes 73736 | tf_op jit(solution)/shard_map/ppermute | solution.py:13
  177.9 42.4 %copy-start.2 = (f32[6,64]{1,0:T(8,128)S(1)}, f32[6,64]{1,0:T(8,128)}, u32[]{:S(2)}) copy-start(f32[6,64]{1,0:T(8,128)} %param.15) | copy-start | bytes 4612
  180.6 3.4 %collective-permute-start.3 = (f32[12,512]{1,0:T(8,128)S(1)}, f32[12,512]{1,0:T(8,128)S(1)}, u32[]{:S(2)}, u32[]{:S(2)}) collective-permute-start(f32[12,512]{1,0:T(8,128)S(1)} %pad_maximum_fusion.3), channel_id=1, source_target_pairs={{0,1},{1,2},{2,3},{3,0},{4,5},{5,6},{6,7},{7,4},{8,9},{9,10},{10,1... | collective-permute-start | bytes 73736 | tf_op jit(solution)/shard_map/ppermute | solution.py:13
  220.2 0.7 copy-start
  220.2 0.6 copy-start.1
where the time goes:
time: 221 us
  blocking collectives  171 us (77%)
  local copies, waits for them, and re-layouts  18.4 us (8%)
  other arithmetic  17.5 us (8%)
  waiting for transfers between devices  8.43 us (4%)
  starting transfers between devices  4.45 us (2%)
    all_gather x1, blocking collectives, per_device(): shard_rows = lax.all_gather(star_table, ('grp', 'blk'), axis=1, tiled=True)  101 us
    psum x1, blocking collectives, per_device(): summed = lax.psum(running, 'grp')  36.1 us
    all_gather x1, blocking collectives, per_device(): group_block = lax.all_gather(own_state, 'grp', axis=1, tiled=True)  33.6 us
    gather x2, local copies, waits for them, and re-layouts, per_device(): jnp.take(shard_rows, jnp.clip(global_id, 0, shard_rows.shape[1] - 1), axi...  15.9 us
    ppermute x4, waiting for transfers between devices, passed_along(): return lax.ppermute(x, axis, [(i, (i + by) % count) for i in range(count)])  8.43 us
    reduce_sum x8, other arithmetic, pair_block(): pull_sum = jnp.sum(weight[None] * separation, axis=2)  5.98 us
    ppermute x4, starting transfers between devices, passed_along(): return lax.ppermute(x, axis, [(i, (i + by) % count) for i in range(count)])  4.45 us
  transfers between devices with their start and end apart: 4, of which 4 were waited for; matrix products, arithmetic and copies ran while one was open for 0% of the time, Pallas kernels for 0%

commit v1 on v0

--- a/solution.py
+++ b/solution.py
@@ -101,7 +101,7 @@
         running = parcel[6:12]
     row_offset = lax.axis_index("grp") * active_rows
     home_state = lax.dynamic_slice_in_dim(moving, row_offset, active_rows, 1)
-    summed = lax.psum(running, "grp")
+    summed = jnp.sum(lax.all_gather(running, "grp"), axis=0)
     regular = lax.dynamic_slice_in_dim(summed, row_offset, active_rows, 1)
     regular = regular / star_total
     return (regular, irregular, corrector(home_state, regular, irregular, old_force))

time: 221 us -> 217 us (0.982)
  blocking collectives: 171 us -> 165 us
    psum x1 -> x0, blocking collectives: 36.1 us -> none  [per_device(): summed = lax.psum(running, 'grp')]
    all_gather x0 -> x1, blocking collectives: none -> 30.5 us  [per_device(): summed = jnp.sum(lax.all_gather(running, 'grp'), axis=0)]
where the time goes in v1:
time: 217 us; the launch traced here: 215 us
  blocking collectives  165 us (76%)
  local copies, waits for them, and re-layouts  18.4 us (8%)
  other arithmetic  17.5 us (8%)
  waiting for transfers between devices  8.43 us (4%)
  starting transfers between devices  4.45 us (2%)
    all_gather x1, blocking collectives, per_device(): shard_rows = lax.all_gather(star_table, ('grp', 'blk'), axis=1, tiled=True)  101 us
    all_gather x1, blocking collectives, per_device(): group_block = lax.all_gather(own_state, 'grp', axis=1, tiled=True)  33.6 us
    all_gather x1, blocking collectives, per_device(): summed = jnp.sum(lax.all_gather(running, 'grp'), axis=0)  30.5 us
    gather x2, local copies, waits for them, and re-layouts, per_device(): jnp.take(shard_rows, jnp.clip(global_id, 0, shard_rows.shape[1] - 1), axi...  15.9 us
    ppermute x4, waiting for transfers between devices, passed_along(): return lax.ppermute(x, axis, [(i, (i + by) % count) for i in range(count)])  8.43 us
    reduce_sum x8, other arithmetic, pair_block(): pull_sum = jnp.sum(weight[None] * separation, axis=2)  5.98 us
    ppermute x4, starting transfers between devices, passed_along(): return lax.ppermute(x, axis, [(i, (i + by) % count) for i in range(count)])  4.45 us
  transfers between devices with their start and end apart: 4, of which 4 were waited for; matrix products, arithmetic and copies ran while one was open for 0% of the time, Pallas kernels for 0%

profile of v1, /device:TPU:0, one launch (start us, length us, event | category | flops | bytes accessed | tf_op | source)
XLA Modules:
  0.0 215.3 jit_solution(4908612185878594898)
XLA Ops:
  0.6 0.8 broadcast_divide_fusion
  1.4 1.4 compare_and_fusion.1
  2.8 0.9 copy.91
  3.8 1.4 compare_and_fusion
  5.2 0.7 pad_maximum_fusion.4
  6.0 0.7 fusion.33
  7.1 0.1 fusion.28
  7.4 101.1 %all_gather.12 = f32[7,16384]{0,1:T(8,128)} all-gather(f32[7,512]{0,1:T(8,128)S(1)} %copy.88), channel_id=1, replica_groups=mesh['grp'=8,'blk'=4] {'grp','blk'}, dimensions={1}, use_global_device_ids=true | all-gather | bytes 473088 | tf_op jit(solution)/shard_map/all_gather | solution.py:87
  108.5 13.9 %gather_fusion = f32[6464,7]{1,0:T(8,128)S(1)} fusion(f32[7,16384]{0,1:T(8,128)} %all_gather.12, s32[7168]{0:T(1024)S(1)} %pad_clamp_fusion), kind=kCustom, calls=%fused_computation | custom fusion | bytes 387840 | tf_op jit(solution)/shard_map/jit(_take)/gather | solution.py:89
  122.4 2.1 copy.92
  124.5 0.7 select_select_fusion
  125.2 0.5 copy.93
  125.7 33.6 %all-gather = f32[6,1,512]{0,1,2:T(1,128)S(1)} all-gather(f32[6,1,64]{0,1,2:T(1,128)S(1)} %copy.93), channel_id=2, replica_groups=mesh['grp'=8,'blk'=4] {'grp'}, dimensions={2}, use_global_device_ids=true | all-gather | bytes 13824 | tf_op jit(solution)/shard_map/all_gather | solution.py:94
  159.5 2.7 %while.36 = (s32[]{:T(128)}, f32[2,6,256]{2,1,0:T(8,128)S(1)}, f32[1,7,512]{2,1,0:T(8,128)S(1)}, f32[2,6,256]{2,0,1:T(2,128)S(1)}, s32[]{:T(128)}, /*index=5*/s32[]{:T(128)}, s32[]{}) while((s32[]{:T(128)}, f32[2,6,256]{2,1,0:T(8,128)S(1)}, f32[1,7,512]{2,1,0:T(8,128)S(1)}, f32[2,6,256]{2,0,1:T(2,128)S(1)}, s32[]{:T(128)}, ...), condition=%wide.region_5.6_spmd, body=%wide.region_0.5_spmd.sunk | while | flops 6029315 | bytes 4309093 | solution.py:45
  159.6 0.4 fusion.46
  160.1 0.7 fusion.47
  160.9 0.4 fusion.46
  161.3 0.1 multiply_divide_fusion.9
  161.5 0.7 fusion.47
  162.4 0.2 multiply_reduce_fusion.3
  162.6 3.0 %collective-permute-done = f32[12,512]{1,0:T(8,128)S(1)} collective-permute-done((f32[12,512]{1,0:T(8,128)S(1)}, f32[12,512]{1,0:T(8,128)S(1)}, u32[]{:S(2)}, u32[]{:S(2)}) %collective-permute-start) | collective-permute-done | bytes 24608 | tf_op jit(solution)/shard_map/ppermute | solution.py:13
  165.6 2.7 %while.37 = (s32[]{:T(128)}, f32[2,6,256]{2,1,0:T(8,128)S(1)}, f32[1,7,512]{2,1,0:T(8,128)S(1)}, f32[2,6,256]{2,1,0:T(8,128)S(1)}, s32[]{:T(128)}, /*index=5*/s32[]{:T(128)}, s32[]{}) while((s32[]{:T(128)}, f32[2,6,256]{2,1,0:T(8,128)S(1)}, f32[1,7,512]{2,1,0:T(8,128)S(1)}, f32[2,6,256]{2,1,0:T(8,128)S(1)}, s32[]{:T(128)}, ...), condition=%wide.region_11.12_spmd, body=%wide.region_6.11_spmd.sunk | while | flops 6029315 | bytes 4296805 | solution.py:45
  165.7 0.4 fusion.49
  166.1 0.1 multiply_divide_fusion.10
  166.2 0.7 fusion.50
  167.0 0.4 fusion.49
  167.4 0.1 multiply_divide_fusion.10
  167.6 0.7 fusion.50
  168.4 1.5 collective-permute-start.1
  169.9 1.8 collective-permute-done.1
  171.8 2.7 %while.38 = (s32[]{:T(128)}, f32[2,6,256]{2,1,0:T(8,128)S(1)}, f32[1,7,512]{2,1,0:T(8,128)S(1)}, f32[2,6,256]{2,1,0:T(8,128)S(1)}, s32[]{:T(128)}, /*index=5*/s32[]{:T(128)}, s32[]{}) while((s32[]{:T(128)}, f32[2,6,256]{2,1,0:T(8,128)S(1)}, f32[1,7,512]{2,1,0:T(8,128)S(1)}, f32[2,6,256]{2,1,0:T(8,128)S(1)}, s32[]{:T(128)}, ...), condition=%wide.region_17.18_spmd, body=%wide.region_12.17_spmd.sunk | while | flops 6029315 | bytes 4296805 | solution.py:45
  171.8 0.4 fusion.52
  172.2 0.1 multiply_divide_fusion.11
  172.3 0.7 fusion.53
  173.1 0.4 fusion.52
  173.7 0.7 fusion.53
  174.5 1.5 collective-permute-start.2
  176.0 1.9 collective-permute-done.2
  177.9 2.7 %while.39 = (s32[]{:T(128)}, f32[2,6,256]{2,1,0:T(8,128)S(1)}, f32[1,7,512]{2,1,0:T(8,128)S(1)}, f32[2,6,256]{2,1,0:T(8,128)S(1)}, s32[]{:T(128)}, /*index=5*/s32[]{:T(128)}, s32[]{}) while((s32[]{:T(128)}, f32[2,6,256]{2,1,0:T(8,128)S(1)}, f32[1,7,512]{2,1,0:T(8,128)S(1)}, f32[2,6,256]{2,1,0:T(8,128)S(1)}, s32[]{:T(128)}, ...), condition=%wide.region_23.24_spmd, body=%wide.region_18.23_spmd.sunk | while | flops 6029315 | bytes 4296805 | solution.py:45
  177.9 0.4 fusion.55
  178.5 0.7 fusion.56
  179.3 0.4 fusion.55
  179.8 0.7 fusion.56
  180.6 1.5 collective-permute-start.3
  182.1 0.2 multiply_reduce_fusion.2
  182.3 1.7 collective-permute-done.3
  184.0 30.5 %all-gather.2 = f32[8,6,512]{2,1,0:T(8,128)S(1)} all-gather(f32[1,6,512]{2,1,0:T(8,128)S(1)} %get-tuple-element.289), channel_id=3, replica_groups=mesh['grp'=8,'blk'=4] {'grp'}, dimensions={0}, use_global_device_ids=true | all-gather | bytes 110592 | tf_op jit(solution)/shard_map/all_gather | solution.py:104
  214.7 0.6 pad_maximum_fusion.5
  (78 shorter events, 2.2 us)
Async XLA Ops:
  162.3 3.4 %collective-permute-start = (f32[12,512]{1,0:T(8,128)S(1)}, f32[12,512]{1,0:T(8,128)S(1)}, u32[]{:S(2)}, u32[]{:S(2)}) collective-permute-start(f32[12,512]{1,0:T(8,128)S(1)} %pad_maximum_fusion), channel_id=1, source_target_pairs={{0,1},{1,2},{2,3},{3,0},{4,5},{5,6},{6,7},{7,4},{8,9},{9,10},{10,1... | collective-permute-start | bytes 73736 | tf_op jit(solution)/shard_map/ppermute | solution.py:13
  168.4 3.4 %collective-permute-start.1 = (f32[12,512]{1,0:T(8,128)S(1)}, f32[12,512]{1,0:T(8,128)S(1)}, u32[]{:S(2)}, u32[]{:S(2)}) collective-permute-start(f32[12,512]{1,0:T(8,128)S(1)} %pad_maximum_fusion.1), channel_id=1, source_target_pairs={{0,1},{1,2},{2,3},{3,0},{4,5},{5,6},{6,7},{7,4},{8,9},{9,10},{10,1... | collective-permute-start | bytes 73736 | tf_op jit(solution)/shard_map/ppermute | solution.py:13
  174.5 3.4 %collective-permute-start.2 = (f32[12,512]{1,0:T(8,128)S(1)}, f32[12,512]{1,0:T(8,128)S(1)}, u32[]{:S(2)}, u32[]{:S(2)}) collective-permute-start(f32[12,512]{1,0:T(8,128)S(1)} %pad_maximum_fusion.2), channel_id=1, source_target_pairs={{0,1},{1,2},{2,3},{3,0},{4,5},{5,6},{6,7},{7,4},{8,9},{9,10},{10,1... | collective-permute-start | bytes 73736 | tf_op jit(solution)/shard_map/ppermute | solution.py:13
  177.9 36.8 %copy-start.2 = (f32[6,64]{1,0:T(8,128)S(1)}, f32[6,64]{1,0:T(8,128)}, u32[]{:S(2)}) copy-start(f32[6,64]{1,0:T(8,128)} %param.15) | copy-start | bytes 4612
  180.6 3.4 %collective-permute-start.3 = (f32[12,512]{1,0:T(8,128)S(1)}, f32[12,512]{1,0:T(8,128)S(1)}, u32[]{:S(2)}, u32[]{:S(2)}) collective-permute-start(f32[12,512]{1,0:T(8,128)S(1)} %pad_maximum_fusion.3), channel_id=1, source_target_pairs={{0,1},{1,2},{2,3},{3,0},{4,5},{5,6},{6,7},{7,4},{8,9},{9,10},{10,1... | collective-permute-start | bytes 73736 | tf_op jit(solution)/shard_map/ppermute | solution.py:13
  214.6 0.7 copy-start
  214.7 0.6 copy-start.1
